TPU v7x, 512 devices: a whole 4x8x8 slice. The times are simulated.
512 devices in a mesh: slab: 32 (over y, x), band: 16 (over z, core).
Axes of the slice: x: 4, y: 8, z: 8, core: 2. Of those that a mesh axis runs over, the one named last changes fastest.
Arguments:
- basis: float32 [3, 512, 49152], P(None, 'slab', 'band')
- offsets: float32 [3, 512, 256], P(None, 'slab', 'band'), may hold values from -0.45 to 0.45
- bond_modulus: float32 [512, 256], P('slab', 'band'), may hold values from 0.5 to 2
- bulk_modulus: float32 [512, 256], P('slab', 'band'), may hold values from 0.5 to 2
- springs: float32 [512, 256], P('slab', 'band'), may hold values from 0.5 to 2
- intact: int32 [32, 32, 9], P('slab', 'band'), may hold values from 0 to 1, as said below
Outputs:
- new_modes: float32 [3, 512, 16384], P(None, 'slab', 'band')
- new_images: float32 [3, 512, 16384], P(None, 'slab', 'band')
- reduced: float32 [64, 64], replicated
Inputs may be any that keep to these rules, and one draw needn't show every extreme that they name: intact[i, j, 3 (dx + 1) + (dy + 1)] is 1 where the bonds between block (i, j) and block (i + dx, j + dy) are intact, and 0 where they are broken or that block lies outside the plate; the entry for (0, 0) is always 1, and the entry for (dx, dy) of one block equals the entry for (-dx, -dy) of the other.
All inputs are finite; a program needn't handle non-finite values.
Results may differ from a plain program's by a relative error of at most 0.0003.
Values sent between devices are 32-bit elements; how exact they have to be, the bound alone decides.
No kernel may reach another device: no remote copies, remote signals or barrier semaphores. Data moves between devices by JAX's collectives and lax.ppermute only.
A program may use at most 128 MiB of HBM per device.

v0:
```python
import jax
import jax.numpy as jnp
from jax import lax
from jax.sharding import PartitionSpec as P

BLOCK_X = 16
BLOCK_Y = 8
REACH = 3
MODES = 64
NCOL = 192
horizon_square = 9.0
bond_scale = 1.0 / 18.0
dilation_scale = 1.0 / 27.0
highest = lax.Precision.HIGHEST


def padded(value, sides, width):
    for axis, dim in sides:
        size, length = (lax.axis_size(axis), value.shape[dim])
        up = [(i, (i + 1) % size) for i in range(size - 1)]
        down = [(j, i) for i, j in up]
        last = lax.slice_in_dim(value, length - width, length, axis=dim)
        first = lax.slice_in_dim(value, 0, width, axis=dim)
        before = lax.ppermute(last, axis, up)
        after = lax.ppermute(first, axis, down)
        value = jnp.concatenate([before, value, after], axis=dim)
    return value


def window(array, margin, region):
    start_x, count_x, start_y, count_y = region
    piece = array[
        :,
        start_x + margin : start_x + margin + count_x,
        start_y + margin : start_y + margin + count_y,
    ]
    return piece.reshape((piece.shape[0], count_x * count_y) + piece.shape[3:])


def widened(region):
    start_x, count_x, start_y, count_y = region
    return (start_x - REACH, count_x + 2 * REACH, start_y - REACH, count_y + 2 * REACH)


def lattice(region):
    start_x, count_x, start_y, count_y = region
    along_x = jnp.repeat(jnp.arange(start_x, start_x + count_x, dtype=jnp.int32), count_y)
    along_y = jnp.tile(jnp.arange(start_y, start_y + count_y, dtype=jnp.int32), count_x)
    return (along_x, along_y)


def pair_geometry(geometry, margin, region, bond_table, table_shift):
    home_geometry = window(geometry, margin, region)
    far_geometry = window(geometry, margin, widened(region))
    home_x, home_y = lattice(region)
    far_x, far_y = lattice(widened(region))
    home_block_x = jnp.floor_divide(home_x, BLOCK_X)
    home_block_y = jnp.floor_divide(home_y, BLOCK_Y)
    offset_code = 3 * (jnp.floor_divide(far_x, BLOCK_X)[None, :] - home_block_x[:, None] + 1) + (
        jnp.floor_divide(far_y, BLOCK_Y)[None, :] - home_block_y[:, None] + 1
    )
    select_rows = (
        home_block_x[:, None] + table_shift
        == jnp.arange(bond_table.shape[0], dtype=jnp.int32)[None, :]
    ).astype(jnp.float32)
    select_cols = (
        home_block_y[:, None] + table_shift
        == jnp.arange(bond_table.shape[1], dtype=jnp.int32)[None, :]
    ).astype(jnp.float32)
    home_bonds = jnp.einsum(
        "na,nb,abo->no", select_rows, select_cols, bond_table.astype(jnp.float32), precision=highest
    )
    intact_mask = jnp.zeros(offset_code.shape, jnp.float32)
    for offset in range(9):
        intact_mask = intact_mask + jnp.where(
            offset_code == offset, home_bonds[:, offset][:, None], 0.0
        )
    bond_vector = jnp.stack(
        [
            (far_x[None, :] - home_x[:, None]).astype(jnp.float32)
            + far_geometry[0][None, :]
            - home_geometry[0][:, None],
            (far_y[None, :] - home_y[:, None]).astype(jnp.float32)
            + far_geometry[1][None, :]
            - home_geometry[1][:, None],
            far_geometry[2][None, :] - home_geometry[2][:, None],
        ],
        axis=1,
    )
    distance = jnp.sum(bond_vector * bond_vector, axis=1)
    weight = jnp.maximum(1.0 - distance / horizon_square, 0.0) * intact_mask
    return (bond_vector, weight, home_geometry, far_geometry)


def volume_terms(tile_set, home_field, far_field):
    bond_vector, weight, home_geometry, far_geometry = tile_set
    home_count = bond_vector.shape[0]
    far_count = bond_vector.shape[2]
    weighted = weight[:, None, :] * bond_vector
    far_flat = far_field.reshape(3 * far_count, home_field.shape[2])
    volume_change = jnp.dot(
        weighted.reshape(home_count, 3 * far_count), far_flat, precision=highest
    )
    return volume_change - jnp.einsum(
        "nc,cnk->nk", jnp.sum(weighted, axis=2), home_field, precision=highest
    )


def bond_terms(tile_set, home_field, far_field):
    bond_vector, weight, home_geometry, far_geometry = tile_set
    home_count = bond_vector.shape[0]
    far_count = bond_vector.shape[2]
    column_count = home_field.shape[2]
    far_flat = far_field.reshape(3 * far_count, column_count)
    coupling = weight * (home_geometry[3][:, None] + far_geometry[3][None, :]) * bond_scale
    leading = jnp.transpose(bond_vector, (1, 0, 2))
    tensor = coupling[None, :, None, :] * leading[:, :, None, :] * bond_vector[None, :, :, :]
    bond_force = jnp.einsum("cnd,dnk->cnk", jnp.sum(tensor, axis=3), home_field, precision=highest)
    return bond_force - jnp.dot(
        tensor.reshape(3 * home_count, 3 * far_count), far_flat, precision=highest
    ).reshape(3, home_count, column_count)


def dilatation_terms(tile_set, home_value, far_value):
    bond_vector, weight, home_geometry, far_geometry = tile_set
    home_count = bond_vector.shape[0]
    weighted = jnp.transpose(weight[:, None, :] * bond_vector, (1, 0, 2))
    remote = jnp.dot(weighted.reshape(3 * home_count, -1), far_value, precision=highest).reshape(
        3, home_count, far_value.shape[1]
    )
    return -(remote + jnp.sum(weighted, axis=2)[:, :, None] * home_value[None, :, :])


def rotation(mass_gram, stiff_gram, mode_count):
    mass_factor = jnp.linalg.cholesky(mass_gram)
    left_solved = lax.linalg.triangular_solve(mass_factor, stiff_gram, left_side=True, lower=True)
    projected = lax.linalg.triangular_solve(mass_factor, left_solved.T, left_side=True, lower=True)
    projected = 0.5 * (projected + projected.T)
    stiff_factor = jnp.linalg.cholesky(projected)
    target = jnp.eye(stiff_gram.shape[0], mode_count, dtype=stiff_gram.dtype)
    forward = lax.linalg.triangular_solve(stiff_factor, target, left_side=True, lower=True)
    inverse = lax.linalg.triangular_solve(
        stiff_factor, forward, left_side=True, lower=True, transpose_a=True
    )
    normal = jnp.linalg.cholesky(jnp.dot(inverse.T, inverse, precision=highest))
    lifted = lax.linalg.triangular_solve(
        mass_factor, inverse, left_side=True, lower=True, transpose_a=True
    )
    return lax.linalg.triangular_solve(
        normal, lifted, left_side=False, lower=True, transpose_a=True
    )


def local(basis, offsets, bond_modulus, bulk_modulus, springs, intact):
    size_x = offsets.shape[1]
    size_y = offsets.shape[2]
    column_count = NCOL
    basis = basis.reshape(3, size_x, size_y, column_count)
    strip_count = intact.shape[0]
    strip_x = size_x // strip_count
    total_rows = float(3 * size_x * size_y * lax.axis_size("slab") * lax.axis_size("band"))
    flat_basis = basis.reshape(-1, column_count)
    strips = [(0, strip_x, 0, size_y)]
    margin = REACH
    geometry = jnp.concatenate([offsets, bond_modulus[None]], axis=0)
    wide_field, wide_geometry = (
        padded(basis, (("slab", 1), ("band", 2)), margin),
        padded(geometry, (("slab", 1), ("band", 2)), margin),
    )
    table_shift = 0
    tile_sets = [
        pair_geometry(wide_geometry, margin, region, intact, table_shift) for region in strips
    ]
    volumes = []
    forces = []
    for region, tile_set in zip(strips, tile_sets):
        home_field = window(wide_field, margin, region)
        far_field = window(wide_field, margin, widened(region))
        volumes.append(volume_terms(tile_set, home_field, far_field))
        forces.append(bond_terms(tile_set, home_field, far_field))
    volume_grid = jnp.concatenate(
        [volume.reshape(strip_x, size_y, column_count) for volume in volumes], axis=0
    )
    dilatation = dilation_scale * bulk_modulus[:, :, None] * volume_grid
    wide_dilatation = padded(dilatation, (("slab", 0), ("band", 1)), REACH)
    images = []
    for region, tile_set, bond_force in zip(strips, tile_sets, forces):
        home_value = window(wide_dilatation[None], REACH, region)[0]
        far_value = window(wide_dilatation[None], REACH, widened(region))[0]
        home_field = window(basis, 0, region)
        stiffness = window(springs[None], 0, region)[0]
        image_strip = (
            bond_force
            + dilatation_terms(tile_set, home_value, far_value)
            + stiffness[None, :, None] * home_field
        )
        images.append(image_strip.reshape(3, strip_x, size_y, column_count))
    image_grid = images[0]
    flat_images = image_grid.reshape(-1, column_count)
    stiff_part = jnp.einsum("rk,rl->kl", flat_basis, flat_images, precision=highest)
    mass_part = jnp.einsum("rk,rl->kl", flat_basis, flat_basis, precision=highest)
    mass_total, stiff_total = lax.psum((mass_part, stiff_part), ("slab", "band"))
    mass_gram = mass_total / total_rows
    stiff_gram = stiff_total / total_rows
    stiff_gram = 0.5 * (stiff_gram + stiff_gram.T)
    rotate = rotation(mass_gram, stiff_gram, MODES)
    new_modes = jnp.einsum("cxyk,km->cxym", basis, rotate, precision=highest)
    new_images = jnp.einsum("cxyk,km->cxym", image_grid, rotate, precision=highest)
    reduced = (
        lax.psum(
            jnp.einsum("cxym,cxyn->mn", new_modes, new_images, precision=highest), ("slab", "band")
        )
        / total_rows
    )
    return (
        new_modes.reshape(3, size_x, size_y * MODES),
        new_images.reshape(3, size_x, size_y * MODES),
        reduced,
    )


def solution(mesh):
    in_specs = (
        P(None, "slab", "band"),
        P(None, "slab", "band"),
        P("slab", "band"),
        P("slab", "band"),
        P("slab", "band"),
        P("slab", "band", None),
    )
    out_specs = (P(None, "slab", "band"), P(None, "slab", "band"), P())
    return jax.shard_map(local, mesh=mesh, in_specs=in_specs, out_specs=out_specs, check_vma=False)
```

profile of v0, /device:TPU:1, one launch (start us, length us, event | category | flops | bytes accessed | tf_op | source)
XLA Modules:
  0.0 619.2 jit_solution(15690530505633483698)
XLA Ops:
  7.2 0.8 pad_maximum_fusion.12
  8.1 1.3 collective-permute-start.1
  9.4 4.6 collective-permute-start
  13.9 1.4 reshape.1000
  15.4 0.7 fusion.90
  16.1 3.4 collective-permute-start.4
  19.5 1.3 collective-permute-start.5
  24.4 2.1 fusion.96
  27.8 7.3 %collective-permute-start.3 = (f32[4,22,3]{2,1,0:T(8,128)}, f32[4,22,3]{2,1,0:T(8,128)S(1)}, u32[]{:S(2)}, u32[]{:S(2)}) collective-permute-start(f32[4,22,3]{2,1,0:T(8,128)} %get-tuple-element.109), channel_id=1, source_target_pairs={{1,0},{2,1},{3,2},{4,3},{5,4},{6,5},{7,6},{8,7},{9,8},{10,9},{11,1... | collective-permute-start | bytes 3176 | tf_op jit(solution)/shard_map/ppermute | solution.py:25
  35.1 1.9 collective-permute-start.2
  38.1 0.8 sub.447
  38.9 0.8 sub.442
  39.6 0.8 sub.434
  40.4 1.1 copy.103
  41.5 1.3 mul.186
  42.9 0.9 pad_maximum_fusion.10
  45.2 0.7 multiply_multiply_fusion
  45.9 1.8 multiply_bitcast_fusion
  47.9 1.0 fusion.89
  48.9 3.0 collective-permute-start.7
  51.9 2.6 collective-permute-start.6
  54.4 0.8 bitcast_reduce_fusion
  55.2 1.2 mul.180
  56.9 1.2 collective-permute-done.6
  58.1 2.8 pad_maximum_fusion
  61.0 2.5 reshape_reshape.16
  63.5 4.4 convolution_subtract_fusion
  68.0 0.8 copy.100
  68.8 1.0 broadcast_multiply_fusion.2
  70.5 1.3 collective-permute-start.9
  71.8 4.9 collective-permute-start.8
  76.7 4.3 fusion.87
  81.0 1.0 copy.96
  82.0 0.7 pad_maximum_fusion.8
  82.7 1.9 collective-permute-start.11
  84.6 4.8 collective-permute-start.10
  89.5 4.3 fusion.19
  93.8 5.4 mul.174
  99.2 2.3 copy.98
  101.5 1.8 fusion.88
  103.3 0.8 squeeze_reshape_broadcast_in_dim.3
  104.2 1.0 slice.333
  105.4 2.5 fusion.16
  107.9 6.6 %fusion.10 = f32[3,256,192]{1,2,0:T(8,128)S(1)} fusion(f32[3,256,192]{1,2,0:T(8,128)S(1)} %fusion.16, f32[3,256,1452]{1,2,0:T(8,128)} %mul.174, f32[1452,192]{1,0:T(8,128)S(1)} %copy-done, f32[256,3,192]{0,2,1:T(8,128)S(1)} %copy-done.5, f32[3,256,192]{1,2,0:T(8,128)S(1)} %copy-done.6, f32[256]{0:T(256)S(1)} %copy-done.23), kind=kOutput, calls=%fused_computation.12 | convolution fusion | flops 2569863168 | bytes 7936000 | tf_op jit(solution)/shard_map/dot_general | solution.py:119
  114.6 2.1 convolution_bitcast_fusion.1
  117.0 275.1 %all-reduce.10.cloned.1.call-done = (f32[192,192]{1,0:T(8,128)}, f32[192,192]{1,0:T(8,128)}) async-done(((f32[192,192]{1,0:T(8,128)}, f32[192,192]{1,0:T(8,128)}), (f32[192,192]{1,0:T(8,128)}, f32[192,192]{1,0:T(8,128)})) %all-reduce.10.cloned.1.call-update) | async-done | bytes 294928 | tf_op jit(solution)/shard_map/psum | solution.py:202
  392.1 1.0 broadcast_multiply_fusion.4
  393.2 1.0 fusion.34
  394.3 11.7 %cholesky.171 = f32[128,128]{1,0:T(8,128)S(1)} custom-call(f32[128,128]{1,0:T(8,128)S(1)} %copy.93), custom_call_target="Cholesky" | custom-call | tf_op jit(solution)/shard_map/jit(cholesky)/cholesky | solution.py:135
  406.1 10.2 %custom-call.28 = f32[1,128,128]{1,2,0:T(8,128)S(1)} custom-call(f32[1,128,128]{2,1,0:T(8,128)S(1)} %get-tuple-element.103), custom_call_target="InvertDiagBlocksLowerTriangular" | custom-call | tf_op jit(solution)/shard_map/jit(cholesky)/cholesky | solution.py:135
  416.8 5.9 cholesky.191
  425.6 19.7 %custom-call.33 = f32[2,128,128]{1,2,0:T(8,128)S(1)} custom-call(f32[2,128,128]{2,1,0:T(8,128)S(1)} %pad_maximum_fusion.4), custom_call_target="InvertDiagBlocksLowerTriangular" | custom-call | tf_op jit(solution)/shard_map/triangular_solve/custom-call.6 | solution.py:146
  447.5 11.7 %cholesky.209 = f32[128,128]{1,0:T(8,128)S(1)} custom-call(f32[128,128]{1,0:T(8,128)S(1)} %cholesky.246), custom_call_target="Cholesky" | custom-call | tf_op jit(solution)/shard_map/jit(cholesky)/cholesky | solution.py:139
  459.2 9.8 %custom-call.31 = f32[1,128,128]{1,2,0:T(8,128)S(1)} custom-call(f32[1,128,128]{2,1,0:T(8,128)S(1)} %get-tuple-element.101), custom_call_target="InvertDiagBlocksLowerTriangular" | custom-call | tf_op jit(solution)/shard_map/jit(cholesky)/cholesky | solution.py:139
  469.4 5.8 cholesky.229
  478.1 19.8 %custom-call.32 = f32[2,128,128]{1,2,0:T(8,128)S(1)} custom-call(f32[2,128,128]{2,1,0:T(8,128)S(1)} %pad_maximum_fusion.5), custom_call_target="InvertDiagBlocksLowerTriangular" | custom-call | tf_op jit(solution)/shard_map/triangular_solve/custom-call.6 | solution.py:142
  500.1 5.8 cholesky.98
  507.3 4.9 custom-call.24
  512.5 0.8 convolution_bitcast_fusion
  513.3 0.8 reshape.1002
  514.1 0.8 fusion.97
  514.9 0.8 reshape.1004
  515.7 0.8 convolution_bitcast_fusion.3
  516.5 95.0 %psum.23 = f32[64,64]{1,0:T(8,128)S(1)} all-reduce(f32[64,64]{1,0:T(8,128)S(1)} %convolution_bitcast_fusion.3), channel_id=1, replica_groups=mesh['slab'=32,'band'=16] {'slab','band'}, use_global_device_ids=true, to_apply=%region_12.16 | all-reduce | flops 4096 | bytes 32768 | tf_op jit(solution)/shard_map/psum | solution.py:210
  (193 shorter events, 19.3 us)
Async XLA Ops:
  7.2 13.6 %copy-start.8 = (f32[3,16,16]{2,1,0:T(8,128)S(1)}, f32[3,16,16]{2,1,0:T(8,128)}, u32[]{:S(2)}) copy-start(f32[3,16,16]{2,1,0:T(8,128)} %param.12) | copy-start | bytes 9220
  7.2 14.2 %copy-start.3 = (f32[3,16,3072]{2,1,0:T(8,128)S(1)}, f32[3,16,3072]{2,1,0:T(8,128)}, u32[]{:S(2)}) copy-start(f32[3,16,3072]{2,1,0:T(8,128)} %param.11) | copy-start | bytes 1769476
  7.2 384.9 %all-reduce.10.cloned.1.call-start = ((), (), s32[]{:S(2)}) async-start(), calls=%async_computation | async-start | bytes 786432 | tf_op jit(solution)/shard_map/psum | solution.py:202
  8.1 19.1 %collective-permute-start.1 = (f32[4,3,16]{2,1,0:T(4,128)S(1)}, f32[4,3,16]{2,1,0:T(4,128)S(1)}, u32[]{:S(2)}, u32[]{:S(2)}) collective-permute-start(f32[4,3,16]{2,1,0:T(4,128)S(1)} %get-tuple-element.115), channel_id=1, source_target_pairs={{16,0},{32,16},{48,32},{64,48},{80,64},{96,80},{112,96},{128,112},... | collective-permute-start | bytes 2312 | tf_op jit(solution)/shard_map/ppermute | solution.py:25
  9.3 13.5 %copy-start.37 = (s32[1,2,9]{2,1,0:T(2,128)S(1)}, s32[1,2,9]{2,1,0:T(2,128)}, u32[]{:S(2)}) copy-start(s32[1,2,9]{2,1,0:T(2,128)} %param.16) | copy-start | bytes 220
  9.3 14.5 %copy-start.22 = (f32[16,16]{1,0:T(8,128)S(1)}, f32[16,16]{1,0:T(8,128)}, u32[]{:S(2)}) copy-start(f32[16,16]{1,0:T(8,128)} %param.14) | copy-start | bytes 3076
  9.4 17.8 %collective-permute-start = (f32[4,3,16]{2,1,0:T(4,128)S(1)}, f32[4,3,16]{2,1,0:T(4,128)S(1)}, u32[]{:S(2)}, u32[]{:S(2)}) collective-permute-start(f32[4,3,16]{2,1,0:T(4,128)S(1)} %get-tuple-element.114), channel_id=1, source_target_pairs={{0,16},{16,32},{32,48},{48,64},{64,80},{80,96},{96,112},{112,128},... | collective-permute-start | bytes 2312 | tf_op jit(solution)/shard_map/ppermute | solution.py:24
  15.4 32.4 %copy-start.1 = (f32[3,16,16,192]{3,2,1,0:T(8,128)}, f32[3,16,16,192]{3,2,1,0:T(8,128)S(1)}, u32[]{:S(2)}) copy-start(f32[3,16,16,192]{3,2,1,0:T(8,128)S(1)} %reshape.1000) | copy-start | bytes 1769476
  16.1 31.6 %collective-permute-start.4 = (f32[3,3,16,192]{3,2,1,0:T(8,128)}, f32[3,3,16,192]{3,2,1,0:T(8,128)S(1)}, u32[]{:S(2)}, u32[]{:S(2)}) collective-permute-start(f32[3,3,16,192]{3,2,1,0:T(8,128)} %get-tuple-element.93), channel_id=1, source_target_pairs={{0,16},{16,32},{32,48},{48,64},{64,80},{80,96},{96,112},{112,128},... | collective-permute-start | bytes 331784 | tf_op jit(solution)/shard_map/ppermute | solution.py:24
  19.5 28.3 %collective-permute-start.5 = (f32[3,3,16,192]{3,2,1,0:T(8,128)S(1)}, f32[3,3,16,192]{3,2,1,0:T(8,128)S(1)}, u32[]{:S(2)}, u32[]{:S(2)}) collective-permute-start(f32[3,3,16,192]{3,2,1,0:T(8,128)S(1)} %get-tuple-element.92), channel_id=1, source_target_pairs={{16,0},{32,16},{48,32},{64,48},{80,64},{96,80},{112,96},{128,112},... | collective-permute-start | bytes 331784 | tf_op jit(solution)/shard_map/ppermute | solution.py:25
  21.4 5.7 copy-start.9
  21.8 5.9 copy-start.18
  22.0 5.8 copy-start.11
  22.1 5.7 copy-start.16
  22.2 5.6 copy-start.13
  22.8 5.0 copy-start.35
  27.1 0.7 copy-start.10
  27.8 15.1 %collective-permute-start.3 = (f32[4,22,3]{2,1,0:T(8,128)}, f32[4,22,3]{2,1,0:T(8,128)S(1)}, u32[]{:S(2)}, u32[]{:S(2)}) collective-permute-start(f32[4,22,3]{2,1,0:T(8,128)} %get-tuple-element.109), channel_id=1, source_target_pairs={{1,0},{2,1},{3,2},{4,3},{5,4},{6,5},{7,6},{8,7},{9,8},{10,9},{11,1... | collective-permute-start | bytes 3176 | tf_op jit(solution)/shard_map/ppermute | solution.py:25
  35.1 7.7 %collective-permute-start.2 = (f32[4,22,3]{2,1,0:T(8,128)S(1)}, f32[4,22,3]{2,1,0:T(8,128)}, u32[]{:S(2)}, u32[]{:S(2)}) collective-permute-start(f32[4,22,3]{2,1,0:T(8,128)S(1)} %get-tuple-element.108), channel_id=1, source_target_pairs={{0,1},{1,2},{2,3},{3,4},{4,5},{5,6},{6,7},{7,8},{8,9},{9,10},{10,1... | collective-permute-start | bytes 3176 | tf_op jit(solution)/shard_map/ppermute | solution.py:24
  38.1 6.3 %copy-start.12 = (s32[484]{0:T(512)S(1)}, s32[484]{0:T(512)}, u32[]{:S(2)}) copy-start(s32[484]{0:T(512)} %copy-done.11) | copy-start | bytes 5812
  38.1 6.3 %copy-start.14 = (s32[484]{0:T(512)S(1)}, s32[484]{0:T(512)}, u32[]{:S(2)}) copy-start(s32[484]{0:T(512)} %copy-done.13) | copy-start | bytes 5812
  38.1 6.3 %copy-start.17 = (s32[256]{0:T(256)S(1)}, s32[256]{0:T(256)}, u32[]{:S(2)}) copy-start(s32[256]{0:T(256)} %copy-done.16) | copy-start | bytes 3076
  38.1 6.3 %copy-start.19 = (s32[256]{0:T(256)S(1)}, s32[256]{0:T(256)}, u32[]{:S(2)}) copy-start(s32[256]{0:T(256)} %copy-done.18) | copy-start | bytes 3076
  44.4 0.7 copy-start.20
  44.4 0.7 copy-start.21
  44.4 0.7 copy-start.24
  44.4 0.7 copy-start.25
  44.4 0.7 copy-start.26
  44.4 0.7 copy-start.27
  44.4 0.7 copy-start.28
  44.4 0.7 copy-start.29
  44.5 0.7 copy-start.30
  44.5 0.7 copy-start.31
  44.5 0.7 copy-start.32
  44.5 0.7 copy-start.33
  44.5 0.7 copy-start.34
  44.5 0.7 copy-start.36
  47.9 6.6 %copy-start.4 = (f32[3,22,16,192]{3,2,1,0:T(8,128)}, f32[3,22,16,192]{3,2,1,0:T(8,128)S(1)}, u32[]{:S(2)}) copy-start(f32[3,22,16,192]{3,2,1,0:T(8,128)S(1)} %constant_dynamic-update-slice_fusion) | copy-start | bytes 2433028
  48.9 8.1 %collective-permute-start.7 = (f32[3,22,3,192]{3,2,1,0:T(4,128)}, f32[3,22,3,192]{3,2,1,0:T(4,128)}, u32[]{:S(2)}, u32[]{:S(2)}) collective-permute-start(f32[3,22,3,192]{3,2,1,0:T(4,128)} %get-tuple-element.91), channel_id=1, source_target_pairs={{1,0},{2,1},{3,2},{4,3},{5,4},{6,5},{7,6},{8,7},{9,8},{10,9},{11,1... | collective-permute-start | bytes 456200 | tf_op jit(solution)/shard_map/ppermute | solution.py:25
  51.9 6.3 %collective-permute-start.6 = (f32[3,22,3,192]{3,2,1,0:T(4,128)}, f32[3,22,3,192]{3,2,1,0:T(4,128)}, u32[]{:S(2)}, u32[]{:S(2)}) collective-permute-start(f32[3,22,3,192]{3,2,1,0:T(4,128)} %get-tuple-element.90), channel_id=1, source_target_pairs={{0,1},{1,2},{2,3},{3,4},{4,5},{5,6},{6,7},{7,8},{8,9},{9,10},{10,1... | collective-permute-start | bytes 456200 | tf_op jit(solution)/shard_map/ppermute | solution.py:24
  70.5 11.5 %collective-permute-start.9 = (f32[3,16,192]{2,1,0:T(8,128)}, f32[3,16,192]{2,1,0:T(8,128)S(1)}, u32[]{:S(2)}, u32[]{:S(2)}) collective-permute-start(f32[3,16,192]{2,1,0:T(8,128)} %get-tuple-element.99), channel_id=1, source_target_pairs={{16,0},{32,16},{48,32},{64,48},{80,64},{96,80},{112,96},{128,112},... | collective-permute-start | bytes 110600 | tf_op jit(solution)/shard_map/ppermute | solution.py:25
  71.8 10.2 %collective-permute-start.8 = (f32[3,16,192]{2,1,0:T(8,128)S(1)}, f32[3,16,192]{2,1,0:T(8,128)S(1)}, u32[]{:S(2)}, u32[]{:S(2)}) collective-permute-start(f32[3,16,192]{2,1,0:T(8,128)S(1)} %get-tuple-element.98), channel_id=1, source_target_pairs={{0,16},{16,32},{32,48},{48,64},{64,80},{80,96},{96,112},{112,128},... | collective-permute-start | bytes 110600 | tf_op jit(solution)/shard_map/ppermute | solution.py:24
  82.7 18.8 %collective-permute-start.11 = (f32[22,3,192]{2,1,0:T(4,128)}, f32[22,3,192]{2,1,0:T(4,128)S(1)}, u32[]{:S(2)}, u32[]{:S(2)}) collective-permute-start(f32[22,3,192]{2,1,0:T(4,128)} %get-tuple-element.97), channel_id=1, source_target_pairs={{1,0},{2,1},{3,2},{4,3},{5,4},{6,5},{7,6},{8,7},{9,8},{10,9},{11,1... | collective-permute-start | bytes 152072 | tf_op jit(solution)/shard_map/ppermute | solution.py:25
  84.6 16.9 %collective-permute-start.10 = (f32[22,3,192]{2,1,0:T(4,128)}, f32[22,3,192]{2,1,0:T(4,128)}, u32[]{:S(2)}, u32[]{:S(2)}) collective-permute-start(f32[22,3,192]{2,1,0:T(4,128)} %get-tuple-element.96), channel_id=1, source_target_pairs={{0,1},{1,2},{2,3},{3,4},{4,5},{5,6},{6,7},{7,8},{8,9},{9,10},{10,1... | collective-permute-start | bytes 152072 | tf_op jit(solution)/shard_map/ppermute | solution.py:24
  101.5 3.9 copy-start.15
  105.3 2.6 copy-start
  105.3 2.6 copy-start.5
  105.3 2.6 copy-start.6
  105.4 2.6 copy-start.23
  392.1 33.2 %copy-start.7 = (f32[192,192]{1,0:T(8,128)S(1)}, f32[192,192]{1,0:T(8,128)}, u32[]{:S(2)}) copy-start(f32[192,192]{1,0:T(8,128)} %get-tuple-element.78) | copy-start | bytes 442372
  459.2 53.3 %copy-start.2 = (f32[3,16,16,192]{3,2,1,0:T(8,128)S(1)}, f32[3,16,16,192]{3,2,1,0:T(8,128)}, u32[]{:S(2)}) copy-start(f32[3,16,16,192]{3,2,1,0:T(8,128)} %copy-done.1) | copy-start | bytes 1769476
Sparse Core Ops, SparseCore 0:
  116.8 275.2 all-reduce.9
where the time goes:
time: 628 us; the launch traced here: 619 us
  waiting for transfers between devices  276 us (44%)
  other arithmetic  131 us (21%)
  blocking collectives  95 us (15%)
  starting transfers between devices  38.3 us (6%)
  local copies, waits for them, and re-layouts  31.2 us (5%)
  matrix products  29.5 us (5%)
  between operations  18 us (3%)
    psum x1, waiting for transfers between devices, local(): lax.psum((mass_part, stiff_part), ('slab', 'band'))  275 us
    psum x1, blocking collectives, local(): lax.psum(jnp.einsum('cxym,cxyn->mn', new_modes, new_images, precision=hig...  95 us
    another operation x7, other arithmetic, rotation(): mass_factor = jnp.linalg.cholesky(mass_gram)  29.1 us
    another operation x7, other arithmetic, rotation(): stiff_factor = jnp.linalg.cholesky(projected)  28.7 us
    ppermute x6, starting transfers between devices, padded(): before = lax.ppermute(last, axis, up)  22.2 us
    another operation x4, other arithmetic, rotation(): lax.linalg.triangular_solve(stiff_factor, forward, left_side=True, lower=...  20 us
    another operation x6, other arithmetic, rotation(): lax.linalg.triangular_solve(mass_factor, inverse, left_side=True, lower=T...  19.8 us
    ppermute x6, starting transfers between devices, padded(): after = lax.ppermute(first, axis, down)  16.1 us
  transfers between devices with their start and end apart: 13, of which 2 were waited for; matrix products, arithmetic and copies ran while one was open for 6% of the time, Pallas kernels for 0%

commit v1 on v0

--- a/solution.py
+++ b/solution.py
@@ -207,8 +207,12 @@
     new_modes = jnp.einsum("cxyk,km->cxym", basis, rotate, precision=highest)
     new_images = jnp.einsum("cxyk,km->cxym", image_grid, rotate, precision=highest)
     reduced = (
-        lax.psum(
-            jnp.einsum("cxym,cxyn->mn", new_modes, new_images, precision=highest), ("slab", "band")
+        jnp.sum(
+            lax.all_gather(
+                jnp.einsum("cxym,cxyn->mn", new_modes, new_images, precision=highest),
+                ("slab", "band"),
+            ),
+            axis=0,
         )
         / total_rows
     )

time: 628 us -> 671 us (1.068)
  waiting for transfers between devices: 276 us -> 412 us
  blocking collectives: 95 us -> 0 us
    all_gather x0 -> x1, waiting for transfers between devices: none -> 129 us  [local(): lax.all_gather(jnp.einsum('cxym,cxyn->mn', new_modes, new_images, precisi...]
    psum x1 -> x0, blocking collectives: 95 us -> none  [local(): lax.psum(jnp.einsum('cxym,cxyn->mn', new_modes, new_images, precision=hig...]
    reduce_sum x0 -> x1, other arithmetic: none -> 6.94 us  [local(): jnp.sum(lax.all_gather(jnp.einsum('cxym,cxyn->mn', new_modes, new_images,...]
  transfers between devices with their start and end apart: 13 -> 14, of which waited for: 2 -> 3; matrix products, arithmetic and copies ran while one was open for 6% -> 6% of each run, Pallas kernels for 0% -> 0%
where the time goes in v1:
time: 671 us; the launch traced here: 662 us
  waiting for transfers between devices  412 us (61%)
  other arithmetic  137 us (20%)
  starting transfers between devices  33.8 us (5%)
  local copies, waits for them, and re-layouts  31.3 us (5%)
  matrix products  30.2 us (5%)
  between operations  18.1 us (3%)
    psum x1, waiting for transfers between devices, local(): lax.psum((mass_part, stiff_part), ('slab', 'band'))  279 us
    all_gather x1, waiting for transfers between devices, local(): lax.all_gather(jnp.einsum('cxym,cxyn->mn', new_modes, new_images, precisi...  129 us
    another operation x7, other arithmetic, rotation(): mass_factor = jnp.linalg.cholesky(mass_gram)  28.7 us
    another operation x7, other arithmetic, rotation(): stiff_factor = jnp.linalg.cholesky(projected)  28.7 us
    ppermute x6, starting transfers between devices, padded(): before = lax.ppermute(last, axis, up)  22.5 us
    another operation x6, other arithmetic, rotation(): lax.linalg.triangular_solve(mass_factor, inverse, left_side=True, lower=T...  20.2 us
    another operation x4, other arithmetic, rotation(): lax.linalg.triangular_solve(stiff_factor, forward, left_side=True, lower=...  20 us
  transfers between devices with their start and end apart: 14, of which 3 were waited for; matrix products, arithmetic and copies ran while one was open for 6% of the time, Pallas kernels for 0%

profile of v1, /device:TPU:1, one launch (start us, length us, event | category | flops | bytes accessed | tf_op | source)
XLA Modules:
  0.0 662.3 jit_solution(5612900749557676077)
XLA Ops:
  7.2 0.8 pad_maximum_fusion.12
  8.1 3.9 collective-permute-start
  12.0 1.3 collective-permute-start.1
  13.3 1.4 reshape.1000
  14.7 0.7 fusion.90
  15.5 1.3 collective-permute-start.5
  16.8 4.6 collective-permute-start.4
  25.5 2.2 fusion.96
  28.9 0.7 fusion.93
  29.6 5.4 collective-permute-start.2
  35.0 2.6 collective-permute-start.3
  38.6 1.3 mul.186
  40.0 0.8 sub.434
  40.7 0.8 sub.447
  41.5 0.8 sub.442
  42.3 1.1 copy.103
  43.4 0.9 pad_maximum_fusion.10
  46.4 1.9 multiply_bitcast_fusion
  48.4 1.0 fusion.89
  49.4 3.0 collective-permute-start.6
  52.3 2.0 collective-permute-start.7
  54.4 0.8 bitcast_reduce_fusion
  55.2 1.2 mul.180
  56.9 3.6 collective-permute-done.7
  60.4 2.8 pad_maximum_fusion
  63.3 2.5 reshape_reshape.16
  65.8 4.4 convolution_subtract_fusion
  70.3 0.8 copy.100
  71.1 1.0 broadcast_multiply_fusion.2
  72.8 3.6 collective-permute-start.8
  76.4 1.3 collective-permute-start.9
  77.7 4.3 fusion.87
  82.0 1.0 copy.96
  83.0 0.7 pad_maximum_fusion.8
  83.7 2.0 collective-permute-start.10
  85.8 2.5 collective-permute-start.11
  88.2 4.3 fusion.19
  92.6 2.3 copy.98
  94.9 5.4 mul.174
  100.3 1.0 fusion.88
  101.5 0.8 squeeze_reshape_broadcast_in_dim.3
  102.3 2.5 fusion.16
  104.9 6.6 fusion.10
  111.5 2.1 convolution_bitcast_fusion.1
  114.2 279.5 %all-reduce.10.cloned.1.call-done = (f32[192,192]{1,0:T(8,128)}, f32[192,192]{1,0:T(8,128)}) async-done(((f32[192,192]{1,0:T(8,128)}, f32[192,192]{1,0:T(8,128)}), (f32[192,192]{1,0:T(8,128)}, f32[192,192]{1,0:T(8,128)})) %all-reduce.10.cloned.1.call-update) | async-done | bytes 294928 | tf_op jit(solution)/shard_map/psum | solution.py:202
  393.7 1.0 broadcast_multiply_fusion.4
  394.8 1.0 fusion.34
  395.9 11.7 %cholesky.171 = f32[128,128]{1,0:T(8,128)S(1)} custom-call(f32[128,128]{1,0:T(8,128)S(1)} %copy.93), custom_call_target="Cholesky" | custom-call | tf_op jit(solution)/shard_map/jit(cholesky)/cholesky | solution.py:135
  408.3 9.8 %custom-call.28 = f32[1,128,128]{1,2,0:T(8,128)S(1)} custom-call(f32[1,128,128]{2,1,0:T(8,128)S(1)} %get-tuple-element.103), custom_call_target="InvertDiagBlocksLowerTriangular" | custom-call | tf_op jit(solution)/shard_map/jit(cholesky)/cholesky | solution.py:135
  418.6 5.9 cholesky.191
  426.8 20.1 %custom-call.33 = f32[2,128,128]{1,2,0:T(8,128)S(1)} custom-call(f32[2,128,128]{2,1,0:T(8,128)S(1)} %pad_maximum_fusion.4), custom_call_target="InvertDiagBlocksLowerTriangular" | custom-call | tf_op jit(solution)/shard_map/triangular_solve/custom-call.6 | solution.py:146
  449.1 11.7 %cholesky.209 = f32[128,128]{1,0:T(8,128)S(1)} custom-call(f32[128,128]{1,0:T(8,128)S(1)} %cholesky.246), custom_call_target="Cholesky" | custom-call | tf_op jit(solution)/shard_map/jit(cholesky)/cholesky | solution.py:139
  461.5 9.8 %custom-call.31 = f32[1,128,128]{1,2,0:T(8,128)S(1)} custom-call(f32[1,128,128]{2,1,0:T(8,128)S(1)} %get-tuple-element.101), custom_call_target="InvertDiagBlocksLowerTriangular" | custom-call | tf_op jit(solution)/shard_map/jit(cholesky)/cholesky | solution.py:139
  471.7 5.8 cholesky.229
  479.7 19.8 %custom-call.32 = f32[2,128,128]{1,2,0:T(8,128)S(1)} custom-call(f32[2,128,128]{2,1,0:T(8,128)S(1)} %pad_maximum_fusion.5), custom_call_target="InvertDiagBlocksLowerTriangular" | custom-call | tf_op jit(solution)/shard_map/triangular_solve/custom-call.6 | solution.py:142
  501.8 5.8 cholesky.98
  508.9 4.9 custom-call.24
  514.1 0.8 convolution_bitcast_fusion
  514.9 0.8 fusion.97
  515.7 1.4 convolution_bitcast_fusion.3
  517.1 0.8 reshape.1002
  518.0 0.8 reshape.1004
  518.8 128.9 %all-gather.3.cloned.1.call-done = f32[32768,64]{1,0:T(8,128)} async-done(((f32[64,64]{1,0:T(8,128)}), f32[32768,64]{1,0:T(8,128)}) %all-gather.3.cloned.1.call-update) | async-done | bytes 8388624 | tf_op jit(solution)/shard_map/all_gather | solution.py:211
  647.7 6.9 %reduce_sum.49 = f32[64,64]{1,0:T(8,128)S(1)} reduce(f32[512,64,64]{2,1,0:T(8,128)} %bitcast.176, f32[]{:T(128)} %constant.183.clone.1), dimensions={0}, to_apply=%region_12.16 | reduce | flops 2093056 | bytes 8404996 | tf_op jit(solution)/shard_map/reduce_sum | solution.py:210
  (196 shorter events, 20.6 us)
Async XLA Ops:
  7.2 14.2 %copy-start.8 = (f32[3,16,16]{2,1,0:T(8,128)S(1)}, f32[3,16,16]{2,1,0:T(8,128)}, u32[]{:S(2)}) copy-start(f32[3,16,16]{2,1,0:T(8,128)} %param.12) | copy-start | bytes 9220
  7.2 14.9 %copy-start.3 = (f32[3,16,3072]{2,1,0:T(8,128)S(1)}, f32[3,16,3072]{2,1,0:T(8,128)}, u32[]{:S(2)}) copy-start(f32[3,16,3072]{2,1,0:T(8,128)} %param.11) | copy-start | bytes 1769476
  7.2 386.5 %all-reduce.10.cloned.1.call-start = ((), (), s32[]{:S(2)}) async-start(), calls=%async_computation.1 | async-start | bytes 786432 | tf_op jit(solution)/shard_map/psum | solution.py:202
  8.1 20.2 %collective-permute-start = (f32[4,3,16]{2,1,0:T(4,128)S(1)}, f32[4,3,16]{2,1,0:T(4,128)S(1)}, u32[]{:S(2)}, u32[]{:S(2)}) collective-permute-start(f32[4,3,16]{2,1,0:T(4,128)S(1)} %get-tuple-element.114), channel_id=1, source_target_pairs={{0,16},{16,32},{32,48},{48,64},{64,80},{80,96},{96,112},{112,128},... | collective-permute-start | bytes 2312 | tf_op jit(solution)/shard_map/ppermute | solution.py:24
  12.0 10.4 %copy-start.22 = (f32[16,16]{1,0:T(8,128)S(1)}, f32[16,16]{1,0:T(8,128)}, u32[]{:S(2)}) copy-start(f32[16,16]{1,0:T(8,128)} %param.14) | copy-start | bytes 3076
  12.0 12.6 %copy-start.37 = (s32[1,2,9]{2,1,0:T(2,128)S(1)}, s32[1,2,9]{2,1,0:T(2,128)}, u32[]{:S(2)}) copy-start(s32[1,2,9]{2,1,0:T(2,128)} %param.16) | copy-start | bytes 220
  12.0 16.2 %collective-permute-start.1 = (f32[4,3,16]{2,1,0:T(4,128)S(1)}, f32[4,3,16]{2,1,0:T(4,128)S(1)}, u32[]{:S(2)}, u32[]{:S(2)}) collective-permute-start(f32[4,3,16]{2,1,0:T(4,128)S(1)} %get-tuple-element.115), channel_id=1, source_target_pairs={{16,0},{32,16},{48,32},{64,48},{80,64},{96,80},{112,96},{128,112},... | collective-permute-start | bytes 2312 | tf_op jit(solution)/shard_map/ppermute | solution.py:25
  14.7 33.5 %copy-start.1 = (f32[3,16,16,192]{3,2,1,0:T(8,128)}, f32[3,16,16,192]{3,2,1,0:T(8,128)S(1)}, u32[]{:S(2)}) copy-start(f32[3,16,16,192]{3,2,1,0:T(8,128)S(1)} %reshape.1000) | copy-start | bytes 1769476
  15.5 32.8 %collective-permute-start.5 = (f32[3,3,16,192]{3,2,1,0:T(8,128)S(1)}, f32[3,3,16,192]{3,2,1,0:T(8,128)S(1)}, u32[]{:S(2)}, u32[]{:S(2)}) collective-permute-start(f32[3,3,16,192]{3,2,1,0:T(8,128)S(1)} %get-tuple-element.92), channel_id=1, source_target_pairs={{16,0},{32,16},{48,32},{64,48},{80,64},{96,80},{112,96},{128,112},... | collective-permute-start | bytes 331784 | tf_op jit(solution)/shard_map/ppermute | solution.py:25
  16.8 31.5 %collective-permute-start.4 = (f32[3,3,16,192]{3,2,1,0:T(8,128)}, f32[3,3,16,192]{3,2,1,0:T(8,128)S(1)}, u32[]{:S(2)}, u32[]{:S(2)}) collective-permute-start(f32[3,3,16,192]{3,2,1,0:T(8,128)} %get-tuple-element.93), channel_id=1, source_target_pairs={{0,16},{16,32},{32,48},{48,64},{64,80},{80,96},{96,112},{112,128},... | collective-permute-start | bytes 331784 | tf_op jit(solution)/shard_map/ppermute | solution.py:24
  22.0 6.8 %copy-start.9 = (f32[16,16]{1,0:T(8,128)S(1)}, f32[16,16]{1,0:T(8,128)}, u32[]{:S(2)}) copy-start(f32[16,16]{1,0:T(8,128)} %param.13) | copy-start | bytes 3076
  23.1 0.5 copy-start.18
  23.6 4.6 copy-start.35
  23.7 4.6 copy-start.16
  24.4 3.9 copy-start.11
  24.5 3.7 copy-start.13
  28.3 0.6 copy-start.10
  29.6 13.8 %collective-permute-start.2 = (f32[4,22,3]{2,1,0:T(8,128)}, f32[4,22,3]{2,1,0:T(8,128)S(1)}, u32[]{:S(2)}, u32[]{:S(2)}) collective-permute-start(f32[4,22,3]{2,1,0:T(8,128)} %get-tuple-element.108), channel_id=1, source_target_pairs={{0,1},{1,2},{2,3},{3,4},{4,5},{5,6},{6,7},{7,8},{8,9},{9,10},{10,1... | collective-permute-start | bytes 3176 | tf_op jit(solution)/shard_map/ppermute | solution.py:24
  35.0 8.4 %collective-permute-start.3 = (f32[4,22,3]{2,1,0:T(8,128)S(1)}, f32[4,22,3]{2,1,0:T(8,128)}, u32[]{:S(2)}, u32[]{:S(2)}) collective-permute-start(f32[4,22,3]{2,1,0:T(8,128)S(1)} %get-tuple-element.109), channel_id=1, source_target_pairs={{1,0},{2,1},{3,2},{4,3},{5,4},{6,5},{7,6},{8,7},{9,8},{10,9},{11,1... | collective-permute-start | bytes 3176 | tf_op jit(solution)/shard_map/ppermute | solution.py:25
  38.6 6.2 copy-start.12
  38.6 6.2 copy-start.14
  38.6 6.2 copy-start.17
  38.6 6.2 copy-start.19
  44.9 0.7 copy-start.20
  44.9 0.7 copy-start.21
  44.9 0.7 copy-start.24
  44.9 0.7 copy-start.25
  44.9 0.7 copy-start.26
  44.9 0.6 copy-start.27
  44.9 0.6 copy-start.28
  44.9 0.6 copy-start.29
  44.9 0.6 copy-start.30
  45.0 0.6 copy-start.31
  45.0 0.6 copy-start.32
  45.0 0.6 copy-start.33
  45.0 0.7 copy-start.34
  45.0 0.7 copy-start.36
  48.3 6.0 copy-start.4
  49.4 7.5 %collective-permute-start.6 = (f32[3,22,3,192]{3,2,1,0:T(4,128)}, f32[3,22,3,192]{3,2,1,0:T(4,128)}, u32[]{:S(2)}, u32[]{:S(2)}) collective-permute-start(f32[3,22,3,192]{3,2,1,0:T(4,128)} %get-tuple-element.90), channel_id=1, source_target_pairs={{0,1},{1,2},{2,3},{3,4},{4,5},{5,6},{6,7},{7,8},{8,9},{9,10},{10,1... | collective-permute-start | bytes 456200 | tf_op jit(solution)/shard_map/ppermute | solution.py:24
  52.3 8.1 %collective-permute-start.7 = (f32[3,22,3,192]{3,2,1,0:T(4,128)}, f32[3,22,3,192]{3,2,1,0:T(4,128)}, u32[]{:S(2)}, u32[]{:S(2)}) collective-permute-start(f32[3,22,3,192]{3,2,1,0:T(4,128)} %get-tuple-element.91), channel_id=1, source_target_pairs={{1,0},{2,1},{3,2},{4,3},{5,4},{6,5},{7,6},{8,7},{9,8},{10,9},{11,1... | collective-permute-start | bytes 456200 | tf_op jit(solution)/shard_map/ppermute | solution.py:25
  72.8 10.3 %collective-permute-start.8 = (f32[3,16,192]{2,1,0:T(8,128)}, f32[3,16,192]{2,1,0:T(8,128)S(1)}, u32[]{:S(2)}, u32[]{:S(2)}) collective-permute-start(f32[3,16,192]{2,1,0:T(8,128)} %get-tuple-element.98), channel_id=1, source_target_pairs={{0,16},{16,32},{32,48},{48,64},{64,80},{80,96},{96,112},{112,128},... | collective-permute-start | bytes 110600 | tf_op jit(solution)/shard_map/ppermute | solution.py:24
  76.4 6.6 %collective-permute-start.9 = (f32[3,16,192]{2,1,0:T(8,128)S(1)}, f32[3,16,192]{2,1,0:T(8,128)S(1)}, u32[]{:S(2)}, u32[]{:S(2)}) collective-permute-start(f32[3,16,192]{2,1,0:T(8,128)S(1)} %get-tuple-element.99), channel_id=1, source_target_pairs={{16,0},{32,16},{48,32},{64,48},{80,64},{96,80},{112,96},{128,112},... | collective-permute-start | bytes 110600 | tf_op jit(solution)/shard_map/ppermute | solution.py:25
  83.7 16.6 %collective-permute-start.10 = (f32[22,3,192]{2,1,0:T(4,128)}, f32[22,3,192]{2,1,0:T(4,128)S(1)}, u32[]{:S(2)}, u32[]{:S(2)}) collective-permute-start(f32[22,3,192]{2,1,0:T(4,128)} %get-tuple-element.96), channel_id=1, source_target_pairs={{0,1},{1,2},{2,3},{3,4},{4,5},{5,6},{6,7},{7,8},{8,9},{9,10},{10,1... | collective-permute-start | bytes 152072 | tf_op jit(solution)/shard_map/ppermute | solution.py:24
  85.8 14.5 %collective-permute-start.11 = (f32[22,3,192]{2,1,0:T(4,128)}, f32[22,3,192]{2,1,0:T(4,128)}, u32[]{:S(2)}, u32[]{:S(2)}) collective-permute-start(f32[22,3,192]{2,1,0:T(4,128)} %get-tuple-element.97), channel_id=1, source_target_pairs={{1,0},{2,1},{3,2},{4,3},{5,4},{6,5},{7,6},{8,7},{9,8},{10,9},{11,1... | collective-permute-start | bytes 152072 | tf_op jit(solution)/shard_map/ppermute | solution.py:25
  100.3 2.0 copy-start.15
  102.3 2.5 copy-start
  102.3 2.5 copy-start.5
  102.3 2.5 copy-start.6
  102.3 2.5 copy-start.23
  113.7 534.0 %all-gather.3.cloned.1.call-start = ((), (), s32[]{:S(2)}) async-start(), calls=%async_computation | async-start | bytes 16809984 | tf_op jit(solution)/shard_map/all_gather | solution.py:211
  393.7 32.8 %copy-start.7 = (f32[192,192]{1,0:T(8,128)S(1)}, f32[192,192]{1,0:T(8,128)}, u32[]{:S(2)}) copy-start(f32[192,192]{1,0:T(8,128)} %get-tuple-element.78) | copy-start | bytes 442372
  460.9 53.3 %copy-start.2 = (f32[3,16,16,192]{3,2,1,0:T(8,128)S(1)}, f32[3,16,16,192]{3,2,1,0:T(8,128)}, u32[]{:S(2)}) copy-start(f32[3,16,16,192]{3,2,1,0:T(8,128)} %copy-done.1) | copy-start | bytes 1769476
Sparse Core Ops, SparseCore 0:
  113.8 279.8 all-reduce.9
  517.3 130.3 all-gather.2
